TPU v7x, 512 devices: a whole 4x4x16 slice. The times are simulated.
512 devices in a mesh: req: 128 (over z_hi, y, x, core), tp: 4 (over z_lo).
Axes of the slice: x: 4, y: 4, z: 16 (z_hi: 4, z_lo: 4; z = z_hi * 4 + z_lo), core: 2. Of those that a mesh axis runs over, the one named last changes fastest.
Arguments:
- queries: bfloat16 [8192, 2560], P('req', 'tp'), may hold values from -20 to 20
- key_values: bfloat16 [8192, 1024], P('req', 'tp'), may hold values from -6 to 6
- hidden: bfloat16 [8192, 2560], P('req'), may hold values from -6 to 6
- lengths: int32 [128, 4], P('req'), may hold values from 1 to 32, 64 in all within a row
- page_table: int32 [128, 4, 2], P('req'), may hold values from 0 to 7, as said below
- out_weight: bfloat16 [2560, 2560], P('tp', 'req'), may hold values from -0.125 to 0.125
- norm_gain: float32 [2560], replicated, may hold values from 0.4 to 1.6
- expert_choice: int32 [8192, 6], P('req'), may hold values from 0 to 63, all different within a row; in each aligned block of 64 rows (0 to 63, 64 to 127, ...) at most 8 rows name the same one
- route_weight: float32 [8192, 6], P('req'), may hold values from 0.05 to 0.5
- gate_up: bfloat16 [128, 2560, 1536], P('req', None, 'tp'), may hold values from -0.125 to 0.125
- down: bfloat16 [128, 768, 2560], P('req', 'tp'), may hold values from -0.15625 to 0.15625
Outputs:
- layer_out: bfloat16 [8192, 2560], P('req', 'tp')
- kv_cache: bfloat16 [1024, 16, 1024], P('req', None, 'tp')
Inputs may be any that keep to these rules, and one draw needn't show every extreme that they name: `expert_choice`: among the 64 rows of one index of req no expert is named by more than 8 rows; the 6 experts of a row differ. `page_table`: the 4 x 2 entries of one index of req are its 8 pool pages, each once.
All inputs are finite; a program needn't handle non-finite values.
Results may differ from a plain program's by a relative error of at most 0.0065.
Values may be sent and summed in bfloat16 or wider, within the bound.
No kernel may reach another device: no remote copies, remote signals or barrier semaphores. Data moves between devices by JAX's collectives and lax.ppermute only.
A program may use at most 64 MiB of HBM per device.

v0:
```python
import jax
import jax.numpy as jnp
from jax import lax
from jax.sharding import PartitionSpec as P

HEAD_DIM = 128
PAGE = 16
epsilon = 1e-05


def prompt_layout(lengths, count):
    ends = jnp.cumsum(lengths)
    starts = ends - lengths
    places = jnp.arange(count, dtype=jnp.int32)
    segment = jnp.sum((ends[None, :] <= places[:, None]).astype(jnp.int32), axis=1)
    picked = segment[:, None] == jnp.arange(lengths.shape[0], dtype=jnp.int32)[None, :]
    offset = places - jnp.sum(jnp.where(picked, starts[None, :], 0), axis=1)
    return (segment, offset)


def attend(queries, key_values, segment):
    count = queries.shape[0]
    local_kv = key_values.shape[1] // (2 * HEAD_DIM)
    local_heads = queries.shape[1] // HEAD_DIM
    group = local_heads // local_kv
    query_rows = queries.reshape(count, local_kv, group, HEAD_DIM)
    key_rows = key_values.reshape(count, local_kv, 2, HEAD_DIM)
    scores = jnp.einsum(
        "qhgd,khd->hgqk", query_rows, key_rows[:, :, 0], preferred_element_type=jnp.float32
    ) * HEAD_DIM ** (-0.5)
    places = jnp.arange(count, dtype=jnp.int32)
    allowed = (segment[:, None] == segment[None, :]) & (places[None, :] <= places[:, None])
    scores = jnp.where(allowed[None, None], scores, -1e30)
    highest = jnp.max(scores, axis=-1, keepdims=True)
    weights = jnp.exp(scores - highest)
    probs = (weights / jnp.sum(weights, axis=-1, keepdims=True)).astype(jnp.bfloat16)
    context = jnp.einsum(
        "hgqk,khd->qhgd", probs, key_rows[:, :, 1], preferred_element_type=jnp.float32
    )
    return context.astype(jnp.bfloat16).reshape(count, local_heads * HEAD_DIM)


def on_device(
    queries,
    key_values,
    hidden,
    lengths,
    page_table,
    out_weight,
    norm_gain,
    expert_choice,
    route_weight,
    gate_up,
    down,
):
    count = queries.shape[0]
    width = hidden.shape[1]
    share = width // lax.axis_size("tp")
    own_start = lax.axis_index("tp") * share
    segment, offset = prompt_layout(lengths[0], count)
    context = attend(queries, key_values, segment)
    attn_part = jnp.dot(
        context,
        lax.all_gather(out_weight, "req", axis=1, tiled=True),
        preferred_element_type=jnp.float32,
    )
    attn = lax.psum(attn_part, "tp")
    mid_full = (hidden.astype(jnp.float32) + attn).astype(jnp.bfloat16)
    mid_wide = lax.optimization_barrier(mid_full).astype(jnp.float32)
    square = jnp.mean(mid_wide * mid_wide, axis=1, keepdims=True)
    normed = (mid_wide * lax.rsqrt(square + epsilon) * norm_gain).astype(jnp.bfloat16)
    mid_own = lax.dynamic_slice_in_dim(mid_wide, own_start, share, 1)
    chosen_count = expert_choice.shape[1]
    experts = lax.axis_size("req") // 2
    capacity = 2 * ((count * chosen_count * 2 + 3 * experts - 1) // (3 * experts))
    flat_choice = expert_choice.reshape(-1)
    hits = (flat_choice[:, None] == jnp.arange(experts, dtype=jnp.int32)[None, :]).astype(jnp.int32)
    ranks = jnp.sum((jnp.cumsum(hits, axis=0) - hits) * hits, axis=1)
    target = flat_choice * capacity + ranks
    onehot = (target[:, None] == jnp.arange(experts * capacity, dtype=jnp.int32)[None, :]).astype(
        jnp.bfloat16
    )
    selector = jnp.sum(onehot.reshape(count, chosen_count, experts * capacity), axis=1)
    outgoing = jnp.dot(selector.T, normed, preferred_element_type=jnp.float32).astype(jnp.bfloat16)
    outgoing = outgoing.reshape(experts, capacity, normed.shape[1])
    gate_up_local = gate_up[0]
    down_local = down[0]
    units = down_local.shape[0]
    doubled = jnp.broadcast_to(outgoing[:, None], (experts, 2, capacity, outgoing.shape[2]))
    doubled = doubled.reshape(2 * experts, capacity, outgoing.shape[2])
    full_rows = lax.all_to_all(doubled, "req", split_axis=0, concat_axis=0, tiled=True)
    senders = full_rows.shape[0]
    items = full_rows.shape[1]
    projected = jnp.dot(
        full_rows.reshape(senders * items, width), gate_up_local, preferred_element_type=jnp.float32
    )
    activated = (jax.nn.silu(projected[:, :units]) * projected[:, units:]).astype(jnp.bfloat16)
    partial_value = jnp.dot(activated, down_local, preferred_element_type=jnp.float32).astype(
        jnp.bfloat16
    )
    incoming = lax.all_to_all(
        partial_value.reshape(senders, items, width), "req", split_axis=0, concat_axis=0, tiled=True
    )
    slot_out = jnp.sum(incoming.reshape(experts, 2, capacity, width).astype(jnp.float32), axis=1)
    slot_out = slot_out.reshape(experts * capacity, width)
    picked = jnp.take(slot_out, target, axis=0).reshape(count, chosen_count, width)
    moe_part = jnp.sum(picked * route_weight[:, :, None], axis=1)
    moe = lax.psum_scatter(
        moe_part.astype(jnp.bfloat16), "tp", scatter_dimension=1, tiled=True
    ).astype(jnp.float32)
    layer_out = (mid_own + moe).astype(jnp.bfloat16)
    pages = page_table[0]
    flat_pages = pages.reshape(-1)
    pool_pages = flat_pages.shape[0]
    page_of = segment * pages.shape[1] + offset // PAGE
    slot_page = jnp.sum(
        jnp.where(
            page_of[:, None] == jnp.arange(pool_pages, dtype=jnp.int32)[None, :],
            flat_pages[None, :],
            0,
        ),
        axis=1,
    )
    cache_rows = slot_page * PAGE + offset % PAGE
    cache = (
        jnp.zeros((pool_pages * PAGE, key_values.shape[1]), jnp.bfloat16)
        .at[cache_rows]
        .set(key_values)
    )
    return (layer_out, cache.reshape(pool_pages, PAGE, key_values.shape[1]))


def solution(mesh):
    placed = (
        P("req", "tp"),
        P("req", "tp"),
        P("req", None),
        P("req", None),
        P("req", None, None),
        P("tp", "req"),
        P(),
        P("req", None),
        P("req", None),
        P("req", None, "tp"),
        P("req", "tp", None),
    )
    return jax.shard_map(
        on_device,
        mesh=mesh,
        in_specs=placed,
        out_specs=(P("req", "tp"), P("req", None, "tp")),
        check_vma=False,
    )
```

profile of v0, /device:TPU:4, one launch (start us, length us, event | category | flops | bytes accessed | tf_op | source)
XLA Modules:
  0.0 765.0 jit_solution(7705690440970895287)
XLA Ops:
  7.2 0.0 copy-start
  7.2 0.0 all-gather.3.cloned.1.call-start
  7.2 0.7 all-gather.3.cloned.1.call-update
  7.9 0.0 all-reduce.2.cloned.1.call-start
  8.0 0.8 reshape.288
  8.7 0.8 reduce-window.10
  9.6 0.1 convert_reduce_fusion.1
  9.7 0.1 fusion.30
  9.8 1.1 fusion.41
  10.9 0.2 fusion.7
  11.2 0.1 copy.57
  11.2 0.8 copy.58
  12.0 0.1 eq.88
  12.1 0.0 copy-start.2
  12.2 0.0 copy-start.1
  12.2 117.9 %all-gather.3.cloned.1.call-done = bf16[128,20,640]{2,1,0:T(8,128)(2,1)} async-done(((bf16[1,20,640]{2,1,0:T(8,128)(2,1)}), bf16[128,20,640]{2,1,0:T(8,128)(2,1)}) %all-gather.3.cloned.1.call-update) | async-done | bytes 3276816 | tf_op jit(solution)/shard_map/all_gather | solution.py:64
  130.1 6.1 reshape.320
  136.2 0.0 copy-start.3
  136.2 3.9 fusion.22
  140.1 0.0 all-reduce.2.cloned.1.call-update
  140.2 0.1 reshape.294
  140.3 0.9 reduce-window.11
  141.2 0.2 slice_reduce_fusion
  141.5 0.1 fusion.20
  141.6 0.1 reduce_sum.93
  141.7 0.1 copy.61
  141.8 0.0 copy-done.2
  141.8 0.1 fusion.11
  142.0 56.9 %all-reduce.2.cloned.1.call-done = f32[64,2560]{1,0:T(8,128)} async-done(((f32[64,2560]{1,0:T(8,128)}), f32[64,2560]{1,0:T(8,128)}) %all-reduce.2.cloned.1.call-update) | async-done | bytes 655376 | tf_op jit(solution)/shard_map/psum | solution.py:67
  198.9 0.0 copy-done.1
  198.9 1.1 add_convert_fusion
  200.1 0.2 multiply_reduce_fusion.1
  200.2 0.0 copy-done.3
  200.3 0.9 fusion.3
  201.2 0.4 broadcast_in_dim.85
  201.6 253.4 %all_to_all.10 = bf16[128,8,2560]{2,1,0:T(8,128)(2,1)S(1)} all-to-all(bf16[128,8,2560]{2,1,0:T(8,128)(2,1)S(1)} %bitcast.109), channel_id=1, replica_groups=mesh['req'=128,'tp'=4] {'req'}, dimensions={0} | all-to-all | bytes 10485760 | tf_op jit(solution)/shard_map/all_to_all | solution.py:91
  454.9 0.0 copy-done
  454.9 2.2 fusion
  457.2 0.0 copy-done.6
  457.2 4.0 fusion.2
  461.1 9.4 %all-to-all-start.1 = ((bf16[128,8,2560]{2,1,0:T(8,128)(2,1)}), bf16[128,8,2560]{2,1,0:T(8,128)(2,1)}, u32[]{:S(2)}, u32[]{:S(2)}) async-start(bf16[128,8,2560]{2,1,0:T(8,128)(2,1)} %fusion.2), calls=%async_computation.1 | async-start | bytes 10485760 | tf_op jit(solution)/shard_map/all_to_all | solution.py:101
  470.6 0.2 reduce-scatter.4.cloned.1.call-start
  470.8 0.1 copy.63
  470.9 0.1 mul.113
  471.1 0.1 copy.62
  471.2 0.0 copy-done.4
  471.2 0.1 copy.64
  471.3 0.0 copy-done.5
  471.3 0.1 copy.65
  471.4 0.1 broadcast_in_dim.91
  471.5 0.0 copy-done.7
  471.5 194.3 %all-to-all-done.1 = bf16[128,8,2560]{2,1,0:T(8,128)(2,1)} async-done(((bf16[128,8,2560]{2,1,0:T(8,128)(2,1)}), bf16[128,8,2560]{2,1,0:T(8,128)(2,1)}, u32[]{:S(2)}, u32[]{:S(2)}) %all-to-all-start.1) | async-done | bytes 5242912 | tf_op jit(solution)/shard_map/all_to_all | solution.py:101
  665.8 6.2 convert_reduce_fusion
  672.0 8.4 %gather_fusion = f32[384,2560]{1,0:T(8,128)} fusion(f32[512,2560]{1,0:T(8,128)} %bitcast.108, s32[1024]{0:T(1024)S(1)} %pad_clamp_fusion), kind=kCustom, calls=%fused_computation | custom fusion | bytes 7865856 | tf_op jit(solution)/shard_map/jit(_take)/gather | solution.py:106
  680.4 5.1 gather.7
  685.5 4.7 multiply_reduce_fusion
  690.3 1.1 copy.67
  691.4 0.0 reduce-scatter.4.cloned.1.call-update
  691.4 0.1 select_reduce_fusion.1
  691.5 0.1 select_reduce_fusion
  691.6 1.6 scatter_custom_fusion
  693.3 63.5 %reduce-scatter.4.cloned.1.call-done = bf16[640,64]{1,0:T(8,128)(2,1)} async-done(((bf16[2560,64]{1,0:T(8,128)(2,1)}), bf16[640,64]{1,0:T(8,128)(2,1)}) %reduce-scatter.4.cloned.1.call-update) | async-done | bytes 81936
  756.8 1.0 copy.68
  757.8 0.7 add_convert_fusion.1
  (17 shorter events, 0.3 us)
Async XLA Ops:
  7.2 447.8 %copy-start = (bf16[1,2560,384]{2,1,0:T(8,128)(2,1)S(1)}, bf16[1,2560,384]{2,1,0:T(8,128)(2,1)}, u32[]{:S(2)}) copy-start(bf16[1,2560,384]{2,1,0:T(8,128)(2,1)} %param.20) | copy-start | bytes 5898244
  7.2 122.9 %all-gather.3.cloned.1.call-start = ((), (), s32[]{:S(2)}) async-start(), calls=%async_computation.4 | async-start | bytes 3962880 | tf_op jit(solution)/shard_map/all_gather | solution.py:64
  7.9 191.0 %all-reduce.2.cloned.1.call-start = ((), (), s32[]{:S(2)}) async-start(), calls=%async_computation.3 | async-start | bytes 1310720 | tf_op jit(solution)/shard_map/psum | solution.py:67
  12.1 129.7 %copy-start.2 = (s32[64,6]{0,1:T(8,128)S(1)}, s32[64,6]{0,1:T(8,128)}, u32[]{:S(2)}) copy-start(s32[64,6]{0,1:T(8,128)} %param.18) | copy-start | bytes 4612
  12.2 186.8 %copy-start.1 = (bf16[64,2560]{1,0:T(8,128)(2,1)S(1)}, bf16[64,2560]{1,0:T(8,128)(2,1)}, u32[]{:S(2)}) copy-start(bf16[64,2560]{1,0:T(8,128)(2,1)} %param.13) | copy-start | bytes 983044
  136.2 64.0 %copy-start.3 = (f32[2560]{0:T(1024)S(1)}, f32[2560]{0:T(1024)}, u32[]{:S(2)}) copy-start(f32[2560]{0:T(1024)} %param.17) | copy-start | bytes 30724
  454.9 2.2 copy-start.6
  461.1 10.0 %copy-start.4 = (f32[64,6]{0,1:T(8,128)S(1)}, f32[64,6]{0,1:T(8,128)}, u32[]{:S(2)}) copy-start(f32[64,6]{0,1:T(8,128)} %param.19) | copy-start | bytes 4612
  461.1 10.1 %copy-start.5 = (s32[1,4,2]{1,2,0:T(2,128)S(1)}, s32[1,4,2]{1,2,0:T(2,128)}, u32[]{:S(2)}) copy-start(s32[1,4,2]{1,2,0:T(2,128)} %param.15) | copy-start | bytes 100
  461.1 10.4 %copy-start.7 = (s32[1,4]{1,0:T(1,128)S(1)}, s32[1,4]{1,0:T(1,128)}, u32[]{:S(2)}) copy-start(s32[1,4]{1,0:T(1,128)} %param.14) | copy-start | bytes 52
  461.1 204.6 %all-to-all-start.1 = ((bf16[128,8,2560]{2,1,0:T(8,128)(2,1)}), bf16[128,8,2560]{2,1,0:T(8,128)(2,1)}, u32[]{:S(2)}, u32[]{:S(2)}) async-start(bf16[128,8,2560]{2,1,0:T(8,128)(2,1)} %fusion.2), calls=%async_computation.1 | async-start | bytes 10485760 | tf_op jit(solution)/shard_map/all_to_all | solution.py:101
  470.6 286.2 %reduce-scatter.4.cloned.1.call-start = ((), (), s32[]{:S(2)}) async-start(), calls=%async_computation.5 | async-start | bytes 819200
Sparse Core Ops, SparseCore 0:
  12.3 117.8 all-gather.2
  140.3 58.6 all-reduce.1
  691.5 65.1 reduce-scatter.3
where the time goes:
time: 766 us; the launch traced here: 765 us
  waiting for transfers between devices  433 us (57%)
  blocking collectives  253 us (33%)
  local copies, waits for them, and re-layouts  26.8 us (3%)
  other arithmetic  15.5 us (2%)
  between operations  13.9 us (2%)
  matrix products  12.3 us (2%)
  starting transfers between devices  9.73 us (1%)
    all_to_all x1, blocking collectives, on_device(): lax.all_to_all(doubled, 'req', split_axis=0, concat_axis=0, tiled=True)  253 us
    all_to_all x1, waiting for transfers between devices, on_device(): lax.all_to_all(partial_value.reshape(senders, items, width), 'req', split...  194 us
    all_gather x1, waiting for transfers between devices, on_device(): lax.all_gather(out_weight, 'req', axis=1, tiled=True)  118 us
    unnamed x4, waiting for transfers between devices  64.2 us
    psum x1, waiting for transfers between devices, on_device(): attn = lax.psum(attn_part, 'tp')  56.9 us
  transfers between devices with their start and end apart: 4, of which 4 were waited for; matrix products, arithmetic and copies ran while one was open for 1% of the time, Pallas kernels for 0%

commit v1 on v0

--- a/solution.py
+++ b/solution.py
@@ -61,7 +61,9 @@
     context = attend(queries, key_values, segment)
     attn_part = jnp.dot(
         context,
-        lax.all_gather(out_weight, "req", axis=1, tiled=True),
+        jnp.concatenate(
+            lax.all_to_all(jnp.stack([out_weight] * lax.axis_size("req")), "req", 0, 0), axis=1
+        ),
         preferred_element_type=jnp.float32,
     )
     attn = lax.psum(attn_part, "tp")

time: 766 us -> 846 us (1.10)
  the two profiles are of different devices: /device:TPU:4 before, /device:TPU:2 now
where the time goes in v1:
time: 846 us; the launch traced here: 845 us
  waiting for transfers between devices  490 us (58%)
  blocking collectives  253 us (30%)
  starting transfers between devices  32.2 us (4%)
  local copies, waits for them, and re-layouts  28.3 us (3%)
  other arithmetic  14.9 us (2%)
  between operations  14.3 us (2%)
  matrix products  11.4 us (1%)
    all_to_all x1, blocking collectives, on_device(): lax.all_to_all(doubled, 'req', split_axis=0, concat_axis=0, tiled=True)  253 us
    all_to_all x1, waiting for transfers between devices, on_device(): lax.all_to_all(partial_value.reshape(senders, items, width), 'req', split...  204 us
    all_to_all x1, waiting for transfers between devices, on_device(): lax.all_to_all(jnp.stack([out_weight] * lax.axis_size('req')), 'req', 0, 0)  175 us
    psum x1, waiting for transfers between devices, on_device(): attn = lax.psum(attn_part, 'tp')  56.9 us
    unnamed x3, waiting for transfers between devices  54.1 us
    all_to_all x1, starting transfers between devices, on_device(): lax.all_to_all(jnp.stack([out_weight] * lax.axis_size('req')), 'req', 0, 0)  22.6 us
  transfers between devices with their start and end apart: 4, of which 4 were waited for; matrix products, arithmetic and copies ran while one was open for 1% of the time, Pallas kernels for 0%

profile of v1, /device:TPU:2, one launch (start us, length us, event | category | flops | bytes accessed | tf_op | source)
XLA Modules:
  0.0 844.7 jit_solution(18265635398694696123)
XLA Ops:
  7.2 0.0 copy-start
  7.2 0.0 copy-start.4
  7.2 0.0 copy-start.9
  7.2 0.0 copy-start.2
  7.2 3.1 stack.2
  10.3 22.6 %all-to-all-start = ((bf16[128,640,20]{1,2,0:T(8,128)(2,1)}), bf16[128,640,20]{1,2,0:T(8,128)(2,1)}, u32[]{:S(2)}, u32[]{:S(2)}) async-start(bf16[128,640,20]{1,2,0:T(8,128)(2,1)} %stack.2), calls=%async_computation | async-start | bytes 7864320 | tf_op jit(solution)/shard_map/all_to_all | solution.py:65
  32.9 0.0 all-reduce.2.cloned.1.call-start
  33.0 0.0 copy-done.4
  33.0 0.0 copy-done.9
  33.0 0.2 reduce-window.10
  33.2 0.1 convert_reduce_fusion.1
  33.3 0.1 fusion.30
  33.4 0.0 copy-done.2
  33.4 0.2 fusion.41
  33.7 0.2 fusion.7
  33.9 0.1 copy.58
  34.0 0.0 copy-done.3
  34.0 0.1 copy.59
  34.1 0.1 eq.88
  34.2 175.3 %all-to-all-done = bf16[128,640,20]{1,2,0:T(8,128)(2,1)} async-done(((bf16[128,640,20]{1,2,0:T(8,128)(2,1)}), bf16[128,640,20]{1,2,0:T(8,128)(2,1)}, u32[]{:S(2)}, u32[]{:S(2)}) %all-to-all-start) | async-done | bytes 3276832 | tf_op jit(solution)/shard_map/all_to_all | solution.py:65
  209.5 6.2 reshape.303
  215.7 3.9 fusion.22
  219.6 0.0 all-reduce.2.cloned.1.call-update
  219.6 0.1 reshape.304
  219.8 0.9 reduce-window.11
  220.7 0.2 slice_reduce_fusion
  220.9 0.1 fusion.20
  221.0 0.1 reduce_sum.93
  221.2 0.1 copy.62
  221.3 0.1 fusion.11
  221.4 56.9 %all-reduce.2.cloned.1.call-done = f32[64,2560]{1,0:T(8,128)} async-done(((f32[64,2560]{1,0:T(8,128)}), f32[64,2560]{1,0:T(8,128)}) %all-reduce.2.cloned.1.call-update) | async-done | bytes 655376 | tf_op jit(solution)/shard_map/psum | solution.py:69
  278.3 0.0 copy-done.1
  278.3 1.1 add_convert_fusion
  279.5 0.2 multiply_reduce_fusion.1
  279.6 0.0 copy-done.5
  279.6 0.9 fusion.3
  280.6 0.4 broadcast_in_dim.85
  281.0 253.4 %all_to_all.15 = bf16[128,8,2560]{2,1,0:T(8,128)(2,1)S(1)} all-to-all(bf16[128,8,2560]{2,1,0:T(8,128)(2,1)S(1)} %bitcast.109), channel_id=1, replica_groups=mesh['req'=128,'tp'=4] {'req'}, dimensions={0} | all-to-all | bytes 10485760 | tf_op jit(solution)/shard_map/all_to_all | solution.py:93
  534.4 0.0 copy-done
  534.4 2.2 fusion
  536.6 0.0 copy-done.8
  536.6 3.9 fusion.2
  540.6 9.5 %all-to-all-start.2 = ((bf16[128,8,2560]{2,1,0:T(8,128)(2,1)}), bf16[128,8,2560]{2,1,0:T(8,128)(2,1)}, u32[]{:S(2)}, u32[]{:S(2)}) async-start(bf16[128,8,2560]{2,1,0:T(8,128)(2,1)} %fusion.2), calls=%async_computation.2 | async-start | bytes 10485760 | tf_op jit(solution)/shard_map/all_to_all | solution.py:103
  550.1 0.0 reduce-scatter.4.cloned.1.call-start
  550.2 0.1 copy.64
  550.3 0.1 mul.113
  550.4 0.1 copy.63
  550.5 0.1 copy.65
  550.6 0.0 copy-done.7
  550.6 0.1 copy.66
  550.7 0.1 broadcast_in_dim.91
  550.9 203.9 %all-to-all-done.2 = bf16[128,8,2560]{2,1,0:T(8,128)(2,1)} async-done(((bf16[128,8,2560]{2,1,0:T(8,128)(2,1)}), bf16[128,8,2560]{2,1,0:T(8,128)(2,1)}, u32[]{:S(2)}, u32[]{:S(2)}) %all-to-all-start.2) | async-done | bytes 5242912 | tf_op jit(solution)/shard_map/all_to_all | solution.py:103
  754.8 6.2 convert_reduce_fusion
  761.0 8.4 gather_fusion
  769.4 5.1 gather.7
  774.5 4.7 multiply_reduce_fusion
  779.3 1.1 copy.68
  780.4 0.0 reduce-scatter.4.cloned.1.call-update
  780.4 0.1 select_reduce_fusion.1
  780.5 0.1 select_reduce_fusion
  780.6 1.4 scatter_custom_fusion
  782.0 54.1 %reduce-scatter.4.cloned.1.call-done = bf16[640,64]{1,0:T(8,128)(2,1)} async-done(((bf16[2560,64]{1,0:T(8,128)(2,1)}), bf16[640,64]{1,0:T(8,128)(2,1)}) %reduce-scatter.4.cloned.1.call-update) | async-done | bytes 81936
  836.1 1.0 copy.69
  837.2 0.7 add_convert_fusion.1
  (21 shorter events, 0.3 us)
Async XLA Ops:
  7.2 527.2 %copy-start = (bf16[1,2560,384]{2,1,0:T(8,128)(2,1)S(1)}, bf16[1,2560,384]{2,1,0:T(8,128)(2,1)}, u32[]{:S(2)}) copy-start(bf16[1,2560,384]{2,1,0:T(8,128)(2,1)} %param.20) | copy-start | bytes 5898244
  7.2 25.8 %copy-start.4 = (bf16[64,256]{1,0:T(8,128)(2,1)S(1)}, bf16[64,256]{1,0:T(8,128)(2,1)}, u32[]{:S(2)}) copy-start(bf16[64,256]{1,0:T(8,128)(2,1)} %param.12) | copy-start | bytes 98308
  7.2 25.8 %copy-start.9 = (s32[1,4]{1,0:T(1,128)S(1)}, s32[1,4]{1,0:T(1,128)}, u32[]{:S(2)}) copy-start(s32[1,4]{1,0:T(1,128)} %param.14) | copy-start | bytes 52
  7.2 26.2 %copy-start.2 = (bf16[64,640]{1,0:T(8,128)(2,1)S(1)}, bf16[64,640]{1,0:T(8,128)(2,1)}, u32[]{:S(2)}) copy-start(bf16[64,640]{1,0:T(8,128)(2,1)} %param.11) | copy-start | bytes 245764
  10.3 23.7 %copy-start.3 = (s32[64,6]{0,1:T(8,128)S(1)}, s32[64,6]{0,1:T(8,128)}, u32[]{:S(2)}) copy-start(s32[64,6]{0,1:T(8,128)} %param.18) | copy-start | bytes 4612
  10.3 199.2 %all-to-all-start = ((bf16[128,640,20]{1,2,0:T(8,128)(2,1)}), bf16[128,640,20]{1,2,0:T(8,128)(2,1)}, u32[]{:S(2)}, u32[]{:S(2)}) async-start(bf16[128,640,20]{1,2,0:T(8,128)(2,1)} %stack.2), calls=%async_computation | async-start | bytes 7864320 | tf_op jit(solution)/shard_map/all_to_all | solution.py:65
  32.9 245.4 %all-reduce.2.cloned.1.call-start = ((), (), s32[]{:S(2)}) async-start(), calls=%async_computation.4 | async-start | bytes 1310720 | tf_op jit(solution)/shard_map/psum | solution.py:69
  209.5 68.8 %copy-start.1 = (bf16[64,2560]{1,0:T(8,128)(2,1)S(1)}, bf16[64,2560]{1,0:T(8,128)(2,1)}, u32[]{:S(2)}) copy-start(bf16[64,2560]{1,0:T(8,128)(2,1)} %param.13) | copy-start | bytes 983044
  215.7 63.9 %copy-start.5 = (f32[2560]{0:T(1024)S(1)}, f32[2560]{0:T(1024)}, u32[]{:S(2)}) copy-start(f32[2560]{0:T(1024)} %param.17) | copy-start | bytes 30724
  534.4 2.2 copy-start.8
  540.6 9.9 %copy-start.6 = (f32[64,6]{0,1:T(8,128)S(1)}, f32[64,6]{0,1:T(8,128)}, u32[]{:S(2)}) copy-start(f32[64,6]{0,1:T(8,128)} %param.19) | copy-start | bytes 4612
  540.6 10.0 %copy-start.7 = (s32[1,4,2]{1,2,0:T(2,128)S(1)}, s32[1,4,2]{1,2,0:T(2,128)}, u32[]{:S(2)}) copy-start(s32[1,4,2]{1,2,0:T(2,128)} %param.15) | copy-start | bytes 100
  540.6 214.2 %all-to-all-start.2 = ((bf16[128,8,2560]{2,1,0:T(8,128)(2,1)}), bf16[128,8,2560]{2,1,0:T(8,128)(2,1)}, u32[]{:S(2)}, u32[]{:S(2)}) async-start(bf16[128,8,2560]{2,1,0:T(8,128)(2,1)} %fusion.2), calls=%async_computation.2 | async-start | bytes 10485760 | tf_op jit(solution)/shard_map/all_to_all | solution.py:103
  550.1 286.0 %reduce-scatter.4.cloned.1.call-start = ((), (), s32[]{:S(2)}) async-start(), calls=%async_computation.5 | async-start | bytes 819200
Sparse Core Ops, SparseCore 0:
  219.7 58.5 all-reduce.1
  780.5 55.5 reduce-scatter.3
